TPU v7x, 256 devices: a whole 4x4x8 slice. The times are simulated.
256 devices in a mesh: seq: 32 (over z, y), mp: 8 (over x, core).
Axes of the slice: x: 4, y: 4, z: 8, core: 2. Of those that a mesh axis runs over, the one named last changes fastest.
Arguments:
- scored_token_targets: int32 [8192], P('seq'), may hold values from 0 to 15999
- valid: int32 [8192], P('seq'), may hold values 0 or 1
- lengths: int32 [48], replicated, may hold values from 1 to 1024, 8192 in all
- owners: int32 [48], replicated, may hold values from 0 to 31
- holders: int32 [48], replicated, may hold values from -1 to 31, as said below
- mixer_input_x: bfloat16 [2, 8192, 3584], P(None, 'seq', 'mp'), may hold values from -6 to 6
- mixer_gate_input: bfloat16 [2, 8192, 3584], P(None, 'seq', 'mp'), may hold values from -6 to 6
- input_projection_b: bfloat16 [2, 8192, 64], P(None, 'seq'), may hold values from -2.390625 to 2.390625
- output_projection_c: bfloat16 [2, 8192, 64], P(None, 'seq'), may hold values from -2.390625 to 2.390625
- token_step_sizes: float32 [2, 8192, 56], P(None, 'seq', 'mp'), may hold values from 0.01 to 0.3
- head_decay_rate: float32 [2, 56], P(None, 'mp'), may hold values from 0.0002 to 1
- head_skip_scale: float32 [2, 56], P(None, 'mp'), may hold values from 0.5 to 1.5
- prompt_held_states: bfloat16 [2, 32, 56, 64, 64], P(None, 'seq', 'mp'), may hold values from -6 to 6
- shared_output_weight: bfloat16 [3584, 3584], P('mp'), may hold values from -0.09375 to 0.09375
- adapter_down_weight: bfloat16 [3584, 128], P('mp'), may hold values from -0.09375 to 0.09375
- adapter_up_weight: bfloat16 [128, 3584], replicated, may hold values from -0.5 to 0.5
- residual: bfloat16 [8192, 2, 3584], P('seq'), may hold values from -16 to 16
- final_norm_scale: float32 [3584], replicated, may hold values from 0.5 to 1.5
- vocab_head_weight: bfloat16 [3584, 16000], P('seq', 'mp'), may hold values from -8 to 8
Outputs:
- owner_sums: float32 [32, 48], P('seq')
- token_delta: float32 [8192], P('seq')
Inputs may be any that keep to these rules, and one draw needn't show every extreme that they name: `holders`: exactly 24 rollouts continue a prompt state; the others start from zeros.
All inputs are finite; a program needn't handle non-finite values. No bound on the sum of `valid` on one device may be relied on, other than what follows from the above.
Results may differ from a plain program's by a relative error of at most 0.035.
Values may be sent and summed in bfloat16 or wider, within the bound.
A program may use at most 128 MiB of HBM per device.

v0:
```python
import jax
import jax.numpy as jnp
from jax import lax
from jax.sharding import PartitionSpec as P

highest = lax.Precision.HIGHEST


def shifted(x, axis, by):
    count = lax.axis_size(axis)
    pairs = [(i, i + by) for i in range(count) if 0 <= i + by < count]
    return lax.ppermute(x, axis, pairs)


def root_norm(hidden, final_norm_scale):
    mean_sq = jnp.mean(hidden * hidden, axis=-1, keepdims=True)
    return (hidden * lax.rsqrt(mean_sq + 1e-05) * final_norm_scale).astype(jnp.bfloat16)


def shards(
    scored_token_targets,
    valid,
    lengths,
    owners,
    holders,
    mixer_input_x,
    mixer_gate_input,
    input_projection_b,
    output_projection_c,
    token_step_sizes,
    head_decay_rate,
    head_skip_scale,
    prompt_held_states,
    shared_output_weight,
    adapter_down_weight,
    adapter_up_weight,
    residual,
    final_norm_scale,
    vocab_head_weight,
):
    seq_count = lax.axis_size("seq")
    mp_count = lax.axis_size("mp")
    tok_rows = scored_token_targets.shape[0]
    models = mixer_input_x.shape[0]
    inner_local = mixer_input_x.shape[2]
    head_count = token_step_sizes.shape[2]
    head_dim = inner_local // head_count
    state_dim = input_projection_b.shape[2]
    roll_count = lengths.shape[0]
    first_row = lax.axis_index("seq") * tok_rows
    offsets = jnp.arange(tok_rows, dtype=jnp.int32)
    position = first_row + offsets
    starts = jnp.cumsum(lengths) - lengths
    rollout = jnp.sum((starts[None, :] <= position[:, None]).astype(jnp.int32), axis=1) - 1
    member_table = rollout[:, None] == jnp.arange(roll_count, dtype=jnp.int32)[None, :]
    start_local = jnp.sum(jnp.where(member_table, starts[None, :], 0), axis=1) - first_row
    holder_tok = jnp.sum(jnp.where(member_table, holders[None, :], 0), axis=1)
    borrowed = (start_local >= 0) & (holder_tok >= 0)
    prompt_pick = (
        (holder_tok[:, None] == jnp.arange(seq_count, dtype=jnp.int32)[None, :]) & borrowed[:, None]
    ).astype(jnp.float32)
    neg_rates = -head_decay_rate
    log_decay = jnp.cumsum(token_step_sizes * neg_rates[:, None, :], axis=1)
    before = jnp.take(log_decay, jnp.maximum(start_local - 1, 0), axis=1)
    before = jnp.where((start_local >= 1)[None, :, None], before, 0.0)
    x_values = mixer_input_x.astype(jnp.float32).reshape(models, tok_rows, head_count, head_dim)
    b_values = input_projection_b.astype(jnp.float32)
    c_values = output_projection_c.astype(jnp.float32)
    gram_matrix = jnp.einsum(
        "mtn,msn->mts", output_projection_c, input_projection_b, preferred_element_type=jnp.float32
    )
    causal = (rollout[:, None] == rollout[None, :]) & (offsets[None, :] <= offsets[:, None])
    log_gap = log_decay[:, :, None, :] - log_decay[:, None, :, :]
    mixing = jnp.where(
        causal[None, :, :, None], jnp.exp(jnp.where(causal[None, :, :, None], log_gap, 0.0)), 0.0
    )
    mixing = mixing * gram_matrix[..., None] * token_step_sizes[:, None, :, :]
    intra_out = jnp.einsum("mtsh,mshp->mthp", mixing, x_values, precision=highest)
    last_pick = prompt_pick[tok_rows - 1]
    zeros_state = jnp.zeros((models, head_count, head_dim, state_dim), jnp.float32)
    piece = lax.all_gather(prompt_held_states, "seq", axis=1, tiled=True)
    last_weight = last_pick.astype(jnp.bfloat16)
    picked = (prompt_pick[None, :, :, None] * c_values[:, :, None, :]).astype(jnp.bfloat16)
    projected = jnp.einsum("mtjn,mjhpn->mthp", picked, piece, preferred_element_type=jnp.float32)
    end_states = jnp.einsum("j,mjhpn->mhpn", last_weight, piece, preferred_element_type=jnp.float32)
    entry_decay = jnp.exp(log_decay - before)
    final_log = log_decay[:, tok_rows - 1, :]
    tail_mask = (rollout == rollout[tok_rows - 1]).astype(jnp.float32)
    end_weight = (
        jnp.exp(final_log[:, None, :] - log_decay) * token_step_sizes * tail_mask[None, :, None]
    )
    local_end = jnp.einsum("msh,mshp,msn->mhpn", end_weight, x_values, b_values, precision=highest)
    local_end = (
        local_end + jnp.exp(final_log - before[:, tok_rows - 1, :])[:, :, None, None] * end_states
    )
    carry_through = jnp.where(start_local[tok_rows - 1] < 0, jnp.exp(final_log), 0.0)

    def relay_step(step_index, incoming):
        outgoing = carry_through[:, :, None, None] * incoming + local_end
        return shifted(outgoing, "seq", 1)

    arriving = lax.fori_loop(0, seq_count - 1, relay_step, zeros_state)
    inherited = (start_local < 0).astype(jnp.float32)
    carried = jnp.einsum("mhpn,mtn->mthp", arriving, c_values, precision=highest)
    carried = carried * (jnp.exp(log_decay) * inherited[None, :, None])[..., None]
    output = (
        intra_out
        + carried
        + entry_decay[..., None] * projected
        + head_skip_scale[:, None, :, None] * x_values
    )
    output = output.reshape(models, tok_rows, inner_local)
    gated_output = (output * jax.nn.silu(mixer_gate_input.astype(jnp.float32))).astype(jnp.bfloat16)
    share_rows = tok_rows // mp_count
    base_output = jnp.einsum(
        "mti,id->tmd", gated_output, shared_output_weight, preferred_element_type=jnp.float32
    )
    low_rank_rows = jnp.dot(
        gated_output[0], adapter_down_weight, preferred_element_type=jnp.float32
    ).astype(jnp.bfloat16)
    adapter_output = jnp.dot(low_rank_rows, adapter_up_weight, preferred_element_type=jnp.float32)
    mixed = lax.psum_scatter(
        jnp.stack([base_output[:, 0] + adapter_output, base_output[:, 1]], axis=1).astype(
            jnp.bfloat16
        ),
        "mp",
        scatter_dimension=0,
        tiled=True,
    ).astype(jnp.float32)
    own_rows = lax.dynamic_slice_in_dim(residual, lax.axis_index("mp") * share_rows, share_rows, 0)
    normed_own = root_norm(own_rows.astype(jnp.float32) + mixed, final_norm_scale)
    normed = lax.all_gather(normed_own, "mp", axis=0, tiled=True)
    vocab_local = vocab_head_weight.shape[1]
    logits = jnp.einsum(
        "tmk,kv->mtv",
        normed,
        lax.all_gather(vocab_head_weight, "seq", axis=0, tiled=True),
        preferred_element_type=jnp.float32,
    )
    vocab_first = lax.axis_index("mp") * vocab_local
    target_hit = (
        scored_token_targets[:, None]
        == vocab_first + jnp.arange(vocab_local, dtype=jnp.int32)[None, :]
    )
    target_local = jnp.sum(jnp.where(target_hit[None], logits, 0.0), axis=2)
    local_max = jnp.max(logits, axis=2)
    vocab_top = lax.pmax(local_max, "mp")
    exp_sums = jnp.sum(jnp.exp(logits - vocab_top[..., None]), axis=2)
    vocab_total, target_logit = lax.psum((exp_sums, target_local), "mp")
    logprob = target_logit - vocab_top - jnp.log(vocab_total)
    token_delta = (logprob[0] - logprob[1]) * valid.astype(jnp.float32)
    roll_sums = jnp.dot(
        token_delta, member_table.astype(jnp.float32), precision=highest
    ) / lengths.astype(jnp.float32)
    owner_rows = (owners[None, :] == jnp.arange(seq_count, dtype=jnp.int32)[:, None]).astype(
        jnp.float32
    ) * roll_sums[None, :]
    owner_sums = lax.psum_scatter(owner_rows, "seq", scatter_dimension=0, tiled=True)
    return (owner_sums, token_delta)


def solution(mesh):
    placed = (
        P("seq"),
        P("seq"),
        P(),
        P(),
        P(),
        P(None, "seq", "mp"),
        P(None, "seq", "mp"),
        P(None, "seq", None),
        P(None, "seq", None),
        P(None, "seq", "mp"),
        P(None, "mp"),
        P(None, "mp"),
        P(None, "seq", "mp", None, None),
        P("mp", None),
        P("mp", None),
        P(),
        P("seq", None, None),
        P(),
        P("seq", "mp"),
    )
    return jax.shard_map(
        shards, mesh=mesh, in_specs=placed, out_specs=(P("seq", None), P("seq")), check_vma=False
    )
```

profile of v0, /device:TPU:0, one launch (start us, length us, event | category | flops | bytes accessed | tf_op | source)
XLA Modules:
  0.0 1076.7 jit_solution(12704770804620089405)
XLA Ops:
  35.8 69.4 %all-gather.4.cloned.1.call-done = bf16[2,32,7,64,64]{4,3,1,2,0:T(8,128)(2,1)} async-done(((bf16[2,1,7,64,64]{4,3,1,2,0:T(8,128)(2,1)}), bf16[2,32,7,64,64]{4,3,1,2,0:T(8,128)(2,1)}) %all-gather.4.cloned.1.call-update) | async-done | bytes 3670032 | tf_op jit(solution)/shard_map/all_gather | solution.py:81
  105.2 7.4 fusion.2
  117.8 498.9 %while.10 = (s32[]{:T(128)}, f32[2,7,64,64]{3,2,1,0:T(8,128)}, f32[2,7]{1,0:T(2,128)S(1)}, f32[2,7,64,64]{3,2,1,0:T(8,128)}, s32[]{:T(128)}) while((s32[]{:T(128)}, f32[2,7,64,64]{3,2,1,0:T(8,128)}, f32[2,7]{1,0:T(2,128)S(1)}, f32[2,7,64,64]{3,2,1,0:T(8,128)}, s32[]{:T(128)}) %tuple.33), condition=%wide.region_7.8_spmd, body=%wide.region_6.7_spmd.sunk | while | flops 114690 | bytes 1605789 | solution.py:102
  122.8 8.9 collective-permute-done
  138.9 7.9 collective-permute-done
  154.1 7.0 collective-permute-done
  215.3 7.3 collective-permute-start
  230.1 7.5 collective-permute-start
  246.1 7.9 collective-permute-start
  254.0 7.5 collective-permute-done
  263.5 8.2 collective-permute-start
  271.7 8.6 collective-permute-done
  282.3 8.2 collective-permute-start
  290.5 9.8 collective-permute-done
  302.4 8.2 collective-permute-start
  310.6 9.9 collective-permute-done
  322.5 7.6 collective-permute-start
  330.1 8.7 collective-permute-done
  347.2 7.4 collective-permute-done
  356.7 7.3 collective-permute-start
  372.5 7.3 collective-permute-start
  387.4 7.3 collective-permute-start
  402.3 7.3 collective-permute-start
  417.1 7.3 collective-permute-start
  431.9 7.3 collective-permute-start
  446.8 7.3 collective-permute-start
  462.2 7.6 collective-permute-start
  469.8 7.1 collective-permute-done
  479.0 8.2 collective-permute-start
  487.1 8.2 collective-permute-done
  497.4 8.2 collective-permute-start
  505.6 9.3 collective-permute-done
  517.0 8.2 collective-permute-start
  525.2 10.3 collective-permute-done
  537.5 7.6 collective-permute-start
  545.1 9.1 collective-permute-done
  556.3 7.1 collective-permute-start
  563.4 8.0 collective-permute-done
  580.2 6.9 collective-permute-done
  589.1 7.3 collective-permute-start
  603.9 7.3 collective-permute-start
  637.7 81.4 %reduce-scatter.2.cloned.1.call-done = bf16[32,2,3584]{2,0,1:T(8,128)(2,1)} async-done(((bf16[256,2,3584]{2,0,1:T(8,128)(2,1)}), bf16[32,2,3584]{2,0,1:T(8,128)(2,1)}) %reduce-scatter.2.cloned.1.call-update) | async-done | bytes 458768 | tf_op jit(solution)/shard_map/reduce_scatter | solution.py:122
  725.5 28.5 %all-gather.6.cloned.1.call-done = bf16[256,2,3584]{2,0,1:T(8,128)(2,1)} async-done(((bf16[32,2,3584]{2,0,1:T(8,128)(2,1)}), bf16[256,2,3584]{2,0,1:T(8,128)(2,1)}) %all-gather.6.cloned.1.call-update) | async-done | bytes 3670032 | tf_op jit(solution)/shard_map/all_gather | solution.py:132
  753.9 132.5 %all-gather.8.cloned.1.call-done = bf16[3584,2000]{1,0:T(8,128)(2,1)} async-done(((bf16[112,2000]{1,0:T(8,128)(2,1)}), bf16[3584,2000]{1,0:T(8,128)(2,1)}) %all-gather.8.cloned.1.call-update) | async-done | bytes 14336016 | tf_op jit(solution)/shard_map/all_gather | solution.py:137
  886.4 13.6 %fusion.6 = (f32[2,256]{1,0:T(2,128)S(1)}, f32[2,256]{1,0:T(2,128)S(1)}, f32[256,2,2000]{0,2,1:T(8,128)}) fusion(pred[256,2000]{0,1:T(8,128)(4,1)} %broadcast_compare_fusion, bf16[256,2,3584]{2,0,1:T(8,128)(2,1)} %all-gather.6.cloned.1.call-done, bf16[3584,2000]{1,0:T(8,128)(2,1)} %all-gather.8.cloned.1.call-done), kind=kOutput, calls=%fused_computation.14 | convolution fusion | flops 7343102976 | bytes 22618112 | tf_op jit(solution)/shard_map/tmk,kv->mtv/dot_general | solution.py:134
  900.0 14.3 %pmax.7 = f32[2,256]{1,0:T(2,128)S(1)} all-reduce(f32[2,256]{1,0:T(2,128)S(1)} %get-tuple-element.26), channel_id=1, replica_groups=mesh['seq'=32,'mp'=8] {'mp'}, use_global_device_ids=true, to_apply=%region_13.14 | all-reduce | flops 512 | bytes 4096 | tf_op jit(solution)/shard_map/pmax | solution.py:147
  917.1 12.4 %all-reduce.1 = (f32[2,256]{1,0:T(2,128)S(1)}, f32[2,256]{1,0:T(2,128)S(1)}) all-reduce(f32[2,256]{1,0:T(2,128)S(1)} %fusion.8, f32[2,256]{1,0:T(2,128)S(1)} %get-tuple-element.25), channel_id=1, replica_groups=mesh['seq'=32,'mp'=8] {'mp'}, use_global_device_ids=true, to_apply=%region_15.16 | all-reduce | flops 1024 | bytes 8192 | tf_op jit(solution)/shard_map/psum | solution.py:149
  929.7 139.3 %all-reduce = f32[32,48]{1,0:T(8,128)S(1)} all-reduce(f32[32,48]{1,0:T(8,128)S(1)} %fusion.54), channel_id=3, replica_groups=mesh['seq'=32,'mp'=8] {'seq'}, use_global_device_ids=true, to_apply=%region_16.17.clone | all-reduce | flops 1536 | bytes 12288
  (173 shorter events, 261.3 us)
Async XLA Ops:
  7.2 613.1 %copy-start = (bf16[448,3584]{1,0:T(8,128)(2,1)S(1)}, bf16[448,3584]{1,0:T(8,128)(2,1)}, u32[]{:S(2)}) copy-start(bf16[448,3584]{1,0:T(8,128)(2,1)} %param.34) | copy-start | bytes 9633796
  7.2 98.0 %all-gather.4.cloned.1.call-start = ((), (), s32[]{:S(2)}) async-start(), calls=%async_computation.1 | async-start | bytes 7569408 | tf_op jit(solution)/shard_map/all_gather | solution.py:81
  7.9 711.2 %reduce-scatter.2.cloned.1.call-start = ((), (), s32[]{:S(2)}) async-start(), calls=%async_computation.2 | async-start | bytes 4128768 | tf_op jit(solution)/shard_map/reduce_scatter | solution.py:122
  30.4 82.1 %copy-start.7 = (bf16[2,256,64]{1,2,0:T(8,128)(2,1)S(1)}, bf16[2,256,64]{1,2,0:T(8,128)(2,1)}, u32[]{:S(2)}) copy-start(bf16[2,256,64]{1,2,0:T(8,128)(2,1)} %param.28) | copy-start | bytes 196612
  105.2 8.8 copy-start.2
  105.2 8.8 copy-start.10
  117.0 499.8 %copy-start.5 = (bf16[2,256,64]{1,2,0:T(8,128)(2,1)S(1)}, bf16[2,256,64]{1,2,0:T(8,128)(2,1)}, u32[]{:S(2)}) copy-start(bf16[2,256,64]{1,2,0:T(8,128)(2,1)} %param.29) | copy-start | bytes 196612
  117.0 499.8 %copy-start.15 = (f32[2,7]{1,0:T(2,128)S(1)}, f32[2,7]{1,0:T(2,128)}, u32[]{:S(2)}) copy-start(f32[2,7]{1,0:T(2,128)} %param.32) | copy-start | bytes 172
  119.9 11.8 %collective-permute-start = (f32[2,7,64,64]{3,2,1,0:T(8,128)}, f32[2,7,64,64]{3,2,1,0:T(8,128)}, u32[]{:S(2)}, u32[]{:S(2)}) collective-permute-start(f32[2,7,64,64]{3,2,1,0:T(8,128)} %multiply_add_fusion.2), channel_id=1, source_target_pairs={{0,8},{8,16},{16,24},{24,32},{32,40},{40,48},{48,56},{56,64},{64,7... | collective-permute-start | bytes 688136 | tf_op jit(solution)/shard_map/while/body/eval_jaxpr/ppermute | solution.py:12
  133.7 13.1 %collective-permute-start = (f32[2,7,64,64]{3,2,1,0:T(8,128)}, f32[2,7,64,64]{3,2,1,0:T(8,128)}, u32[]{:S(2)}, u32[]{:S(2)}) collective-permute-start(f32[2,7,64,64]{3,2,1,0:T(8,128)} %multiply_add_fusion.2), channel_id=1, source_target_pairs={{0,8},{8,16},{16,24},{24,32},{32,40},{40,48},{48,56},{56,64},{64,7... | collective-permute-start | bytes 688136 | tf_op jit(solution)/shard_map/while/body/eval_jaxpr/ppermute | solution.py:12
  148.9 12.2 %collective-permute-start = (f32[2,7,64,64]{3,2,1,0:T(8,128)}, f32[2,7,64,64]{3,2,1,0:T(8,128)}, u32[]{:S(2)}, u32[]{:S(2)}) collective-permute-start(f32[2,7,64,64]{3,2,1,0:T(8,128)} %multiply_add_fusion.2), channel_id=1, source_target_pairs={{0,8},{8,16},{16,24},{24,32},{32,40},{40,48},{48,56},{56,64},{64,7... | collective-permute-start | bytes 688136 | tf_op jit(solution)/shard_map/while/body/eval_jaxpr/ppermute | solution.py:12
  163.1 11.3 %collective-permute-start = (f32[2,7,64,64]{3,2,1,0:T(8,128)}, f32[2,7,64,64]{3,2,1,0:T(8,128)}, u32[]{:S(2)}, u32[]{:S(2)}) collective-permute-start(f32[2,7,64,64]{3,2,1,0:T(8,128)} %multiply_add_fusion.2), channel_id=1, source_target_pairs={{0,8},{8,16},{16,24},{24,32},{32,40},{40,48},{48,56},{56,64},{64,7... | collective-permute-start | bytes 688136 | tf_op jit(solution)/shard_map/while/body/eval_jaxpr/ppermute | solution.py:12
  176.4 10.7 collective-permute-start
  189.2 10.7 collective-permute-start
  201.9 11.4 %collective-permute-start = (f32[2,7,64,64]{3,2,1,0:T(8,128)}, f32[2,7,64,64]{3,2,1,0:T(8,128)}, u32[]{:S(2)}, u32[]{:S(2)}) collective-permute-start(f32[2,7,64,64]{3,2,1,0:T(8,128)} %multiply_add_fusion.2), channel_id=1, source_target_pairs={{0,8},{8,16},{16,24},{24,32},{32,40},{40,48},{48,56},{56,64},{64,7... | collective-permute-start | bytes 688136 | tf_op jit(solution)/shard_map/while/body/eval_jaxpr/ppermute | solution.py:12
  215.3 12.8 %collective-permute-start = (f32[2,7,64,64]{3,2,1,0:T(8,128)}, f32[2,7,64,64]{3,2,1,0:T(8,128)}, u32[]{:S(2)}, u32[]{:S(2)}) collective-permute-start(f32[2,7,64,64]{3,2,1,0:T(8,128)} %multiply_add_fusion.2), channel_id=1, source_target_pairs={{0,8},{8,16},{16,24},{24,32},{32,40},{40,48},{48,56},{56,64},{64,7... | collective-permute-start | bytes 688136 | tf_op jit(solution)/shard_map/while/body/eval_jaxpr/ppermute | solution.py:12
  230.1 13.9 %collective-permute-start = (f32[2,7,64,64]{3,2,1,0:T(8,128)}, f32[2,7,64,64]{3,2,1,0:T(8,128)}, u32[]{:S(2)}, u32[]{:S(2)}) collective-permute-start(f32[2,7,64,64]{3,2,1,0:T(8,128)} %multiply_add_fusion.2), channel_id=1, source_target_pairs={{0,8},{8,16},{16,24},{24,32},{32,40},{40,48},{48,56},{56,64},{64,7... | collective-permute-start | bytes 688136 | tf_op jit(solution)/shard_map/while/body/eval_jaxpr/ppermute | solution.py:12
  246.1 15.4 %collective-permute-start = (f32[2,7,64,64]{3,2,1,0:T(8,128)}, f32[2,7,64,64]{3,2,1,0:T(8,128)}, u32[]{:S(2)}, u32[]{:S(2)}) collective-permute-start(f32[2,7,64,64]{3,2,1,0:T(8,128)} %multiply_add_fusion.2), channel_id=1, source_target_pairs={{0,8},{8,16},{16,24},{24,32},{32,40},{40,48},{48,56},{56,64},{64,7... | collective-permute-start | bytes 688136 | tf_op jit(solution)/shard_map/while/body/eval_jaxpr/ppermute | solution.py:12
  263.5 16.8 %collective-permute-start = (f32[2,7,64,64]{3,2,1,0:T(8,128)}, f32[2,7,64,64]{3,2,1,0:T(8,128)}, u32[]{:S(2)}, u32[]{:S(2)}) collective-permute-start(f32[2,7,64,64]{3,2,1,0:T(8,128)} %multiply_add_fusion.2), channel_id=1, source_target_pairs={{0,8},{8,16},{16,24},{24,32},{32,40},{40,48},{48,56},{56,64},{64,7... | collective-permute-start | bytes 688136 | tf_op jit(solution)/shard_map/while/body/eval_jaxpr/ppermute | solution.py:12
  282.3 18.0 %collective-permute-start = (f32[2,7,64,64]{3,2,1,0:T(8,128)}, f32[2,7,64,64]{3,2,1,0:T(8,128)}, u32[]{:S(2)}, u32[]{:S(2)}) collective-permute-start(f32[2,7,64,64]{3,2,1,0:T(8,128)} %multiply_add_fusion.2), channel_id=1, source_target_pairs={{0,8},{8,16},{16,24},{24,32},{32,40},{40,48},{48,56},{56,64},{64,7... | collective-permute-start | bytes 688136 | tf_op jit(solution)/shard_map/while/body/eval_jaxpr/ppermute | solution.py:12
  302.4 18.1 %collective-permute-start = (f32[2,7,64,64]{3,2,1,0:T(8,128)}, f32[2,7,64,64]{3,2,1,0:T(8,128)}, u32[]{:S(2)}, u32[]{:S(2)}) collective-permute-start(f32[2,7,64,64]{3,2,1,0:T(8,128)} %multiply_add_fusion.2), channel_id=1, source_target_pairs={{0,8},{8,16},{16,24},{24,32},{32,40},{40,48},{48,56},{56,64},{64,7... | collective-permute-start | bytes 688136 | tf_op jit(solution)/shard_map/while/body/eval_jaxpr/ppermute | solution.py:12
  322.5 16.2 %collective-permute-start = (f32[2,7,64,64]{3,2,1,0:T(8,128)}, f32[2,7,64,64]{3,2,1,0:T(8,128)}, u32[]{:S(2)}, u32[]{:S(2)}) collective-permute-start(f32[2,7,64,64]{3,2,1,0:T(8,128)} %multiply_add_fusion.2), channel_id=1, source_target_pairs={{0,8},{8,16},{16,24},{24,32},{32,40},{40,48},{48,56},{56,64},{64,7... | collective-permute-start | bytes 688136 | tf_op jit(solution)/shard_map/while/body/eval_jaxpr/ppermute | solution.py:12
  340.8 13.8 %collective-permute-start = (f32[2,7,64,64]{3,2,1,0:T(8,128)}, f32[2,7,64,64]{3,2,1,0:T(8,128)}, u32[]{:S(2)}, u32[]{:S(2)}) collective-permute-start(f32[2,7,64,64]{3,2,1,0:T(8,128)} %multiply_add_fusion.2), channel_id=1, source_target_pairs={{0,8},{8,16},{16,24},{24,32},{32,40},{40,48},{48,56},{56,64},{64,7... | collective-permute-start | bytes 688136 | tf_op jit(solution)/shard_map/while/body/eval_jaxpr/ppermute | solution.py:12
  356.7 13.8 %collective-permute-start = (f32[2,7,64,64]{3,2,1,0:T(8,128)}, f32[2,7,64,64]{3,2,1,0:T(8,128)}, u32[]{:S(2)}, u32[]{:S(2)}) collective-permute-start(f32[2,7,64,64]{3,2,1,0:T(8,128)} %multiply_add_fusion.2), channel_id=1, source_target_pairs={{0,8},{8,16},{16,24},{24,32},{32,40},{40,48},{48,56},{56,64},{64,7... | collective-permute-start | bytes 688136 | tf_op jit(solution)/shard_map/while/body/eval_jaxpr/ppermute | solution.py:12
  372.5 12.9 %collective-permute-start = (f32[2,7,64,64]{3,2,1,0:T(8,128)}, f32[2,7,64,64]{3,2,1,0:T(8,128)}, u32[]{:S(2)}, u32[]{:S(2)}) collective-permute-start(f32[2,7,64,64]{3,2,1,0:T(8,128)} %multiply_add_fusion.2), channel_id=1, source_target_pairs={{0,8},{8,16},{16,24},{24,32},{32,40},{40,48},{48,56},{56,64},{64,7... | collective-permute-start | bytes 688136 | tf_op jit(solution)/shard_map/while/body/eval_jaxpr/ppermute | solution.py:12
  387.4 12.8 %collective-permute-start = (f32[2,7,64,64]{3,2,1,0:T(8,128)}, f32[2,7,64,64]{3,2,1,0:T(8,128)}, u32[]{:S(2)}, u32[]{:S(2)}) collective-permute-start(f32[2,7,64,64]{3,2,1,0:T(8,128)} %multiply_add_fusion.2), channel_id=1, source_target_pairs={{0,8},{8,16},{16,24},{24,32},{32,40},{40,48},{48,56},{56,64},{64,7... | collective-permute-start | bytes 688136 | tf_op jit(solution)/shard_map/while/body/eval_jaxpr/ppermute | solution.py:12
  402.3 12.8 %collective-permute-start = (f32[2,7,64,64]{3,2,1,0:T(8,128)}, f32[2,7,64,64]{3,2,1,0:T(8,128)}, u32[]{:S(2)}, u32[]{:S(2)}) collective-permute-start(f32[2,7,64,64]{3,2,1,0:T(8,128)} %multiply_add_fusion.2), channel_id=1, source_target_pairs={{0,8},{8,16},{16,24},{24,32},{32,40},{40,48},{48,56},{56,64},{64,7... | collective-permute-start | bytes 688136 | tf_op jit(solution)/shard_map/while/body/eval_jaxpr/ppermute | solution.py:12
  417.1 12.8 %collective-permute-start = (f32[2,7,64,64]{3,2,1,0:T(8,128)}, f32[2,7,64,64]{3,2,1,0:T(8,128)}, u32[]{:S(2)}, u32[]{:S(2)}) collective-permute-start(f32[2,7,64,64]{3,2,1,0:T(8,128)} %multiply_add_fusion.2), channel_id=1, source_target_pairs={{0,8},{8,16},{16,24},{24,32},{32,40},{40,48},{48,56},{56,64},{64,7... | collective-permute-start | bytes 688136 | tf_op jit(solution)/shard_map/while/body/eval_jaxpr/ppermute | solution.py:12
  431.9 12.8 %collective-permute-start = (f32[2,7,64,64]{3,2,1,0:T(8,128)}, f32[2,7,64,64]{3,2,1,0:T(8,128)}, u32[]{:S(2)}, u32[]{:S(2)}) collective-permute-start(f32[2,7,64,64]{3,2,1,0:T(8,128)} %multiply_add_fusion.2), channel_id=1, source_target_pairs={{0,8},{8,16},{16,24},{24,32},{32,40},{40,48},{48,56},{56,64},{64,7... | collective-permute-start | bytes 688136 | tf_op jit(solution)/shard_map/while/body/eval_jaxpr/ppermute | solution.py:12
  446.8 13.4 %collective-permute-start = (f32[2,7,64,64]{3,2,1,0:T(8,128)}, f32[2,7,64,64]{3,2,1,0:T(8,128)}, u32[]{:S(2)}, u32[]{:S(2)}) collective-permute-start(f32[2,7,64,64]{3,2,1,0:T(8,128)} %multiply_add_fusion.2), channel_id=1, source_target_pairs={{0,8},{8,16},{16,24},{24,32},{32,40},{40,48},{48,56},{56,64},{64,7... | collective-permute-start | bytes 688136 | tf_op jit(solution)/shard_map/while/body/eval_jaxpr/ppermute | solution.py:12
  462.2 14.7 %collective-permute-start = (f32[2,7,64,64]{3,2,1,0:T(8,128)}, f32[2,7,64,64]{3,2,1,0:T(8,128)}, u32[]{:S(2)}, u32[]{:S(2)}) collective-permute-start(f32[2,7,64,64]{3,2,1,0:T(8,128)} %multiply_add_fusion.2), channel_id=1, source_target_pairs={{0,8},{8,16},{16,24},{24,32},{32,40},{40,48},{48,56},{56,64},{64,7... | collective-permute-start | bytes 688136 | tf_op jit(solution)/shard_map/while/body/eval_jaxpr/ppermute | solution.py:12
  479.0 16.4 %collective-permute-start = (f32[2,7,64,64]{3,2,1,0:T(8,128)}, f32[2,7,64,64]{3,2,1,0:T(8,128)}, u32[]{:S(2)}, u32[]{:S(2)}) collective-permute-start(f32[2,7,64,64]{3,2,1,0:T(8,128)} %multiply_add_fusion.2), channel_id=1, source_target_pairs={{0,8},{8,16},{16,24},{24,32},{32,40},{40,48},{48,56},{56,64},{64,7... | collective-permute-start | bytes 688136 | tf_op jit(solution)/shard_map/while/body/eval_jaxpr/ppermute | solution.py:12
  497.4 17.5 %collective-permute-start = (f32[2,7,64,64]{3,2,1,0:T(8,128)}, f32[2,7,64,64]{3,2,1,0:T(8,128)}, u32[]{:S(2)}, u32[]{:S(2)}) collective-permute-start(f32[2,7,64,64]{3,2,1,0:T(8,128)} %multiply_add_fusion.2), channel_id=1, source_target_pairs={{0,8},{8,16},{16,24},{24,32},{32,40},{40,48},{48,56},{56,64},{64,7... | collective-permute-start | bytes 688136 | tf_op jit(solution)/shard_map/while/body/eval_jaxpr/ppermute | solution.py:12
  517.0 18.5 %collective-permute-start = (f32[2,7,64,64]{3,2,1,0:T(8,128)}, f32[2,7,64,64]{3,2,1,0:T(8,128)}, u32[]{:S(2)}, u32[]{:S(2)}) collective-permute-start(f32[2,7,64,64]{3,2,1,0:T(8,128)} %multiply_add_fusion.2), channel_id=1, source_target_pairs={{0,8},{8,16},{16,24},{24,32},{32,40},{40,48},{48,56},{56,64},{64,7... | collective-permute-start | bytes 688136 | tf_op jit(solution)/shard_map/while/body/eval_jaxpr/ppermute | solution.py:12
  537.5 16.7 %collective-permute-start = (f32[2,7,64,64]{3,2,1,0:T(8,128)}, f32[2,7,64,64]{3,2,1,0:T(8,128)}, u32[]{:S(2)}, u32[]{:S(2)}) collective-permute-start(f32[2,7,64,64]{3,2,1,0:T(8,128)} %multiply_add_fusion.2), channel_id=1, source_target_pairs={{0,8},{8,16},{16,24},{24,32},{32,40},{40,48},{48,56},{56,64},{64,7... | collective-permute-start | bytes 688136 | tf_op jit(solution)/shard_map/while/body/eval_jaxpr/ppermute | solution.py:12
  556.3 15.0 %collective-permute-start = (f32[2,7,64,64]{3,2,1,0:T(8,128)}, f32[2,7,64,64]{3,2,1,0:T(8,128)}, u32[]{:S(2)}, u32[]{:S(2)}) collective-permute-start(f32[2,7,64,64]{3,2,1,0:T(8,128)} %multiply_add_fusion.2), channel_id=1, source_target_pairs={{0,8},{8,16},{16,24},{24,32},{32,40},{40,48},{48,56},{56,64},{64,7... | collective-permute-start | bytes 688136 | tf_op jit(solution)/shard_map/while/body/eval_jaxpr/ppermute | solution.py:12
  573.4 13.7 %collective-permute-start = (f32[2,7,64,64]{3,2,1,0:T(8,128)}, f32[2,7,64,64]{3,2,1,0:T(8,128)}, u32[]{:S(2)}, u32[]{:S(2)}) collective-permute-start(f32[2,7,64,64]{3,2,1,0:T(8,128)} %multiply_add_fusion.2), channel_id=1, source_target_pairs={{0,8},{8,16},{16,24},{24,32},{32,40},{40,48},{48,56},{56,64},{64,7... | collective-permute-start | bytes 688136 | tf_op jit(solution)/shard_map/while/body/eval_jaxpr/ppermute | solution.py:12
  589.1 12.8 %collective-permute-start = (f32[2,7,64,64]{3,2,1,0:T(8,128)}, f32[2,7,64,64]{3,2,1,0:T(8,128)}, u32[]{:S(2)}, u32[]{:S(2)}) collective-permute-start(f32[2,7,64,64]{3,2,1,0:T(8,128)} %multiply_add_fusion.2), channel_id=1, source_target_pairs={{0,8},{8,16},{16,24},{24,32},{32,40},{40,48},{48,56},{56,64},{64,7... | collective-permute-start | bytes 688136 | tf_op jit(solution)/shard_map/while/body/eval_jaxpr/ppermute | solution.py:12
  603.9 12.8 %collective-permute-start = (f32[2,7,64,64]{3,2,1,0:T(8,128)}, f32[2,7,64,64]{3,2,1,0:T(8,128)}, u32[]{:S(2)}, u32[]{:S(2)}) collective-permute-start(f32[2,7,64,64]{3,2,1,0:T(8,128)} %multiply_add_fusion.2), channel_id=1, source_target_pairs={{0,8},{8,16},{16,24},{24,32},{32,40},{40,48},{48,56},{56,64},{64,7... | collective-permute-start | bytes 688136 | tf_op jit(solution)/shard_map/while/body/eval_jaxpr/ppermute | solution.py:12
  635.5 85.0 %copy-start.9 = (f32[3584]{0:T(1024)S(1)}, f32[3584]{0:T(1024)}, u32[]{:S(2)}) copy-start(f32[3584]{0:T(1024)} %param.38) | copy-start | bytes 43012
  635.5 87.7 %copy-start.18 = (u32[256]{0:T(256)S(1)}, u32[256]{0:T(256)}, u32[]{:S(2)}) copy-start(u32[256]{0:T(256)} %constant.72) | copy-start | bytes 3076
  635.5 88.3 %copy-start.12 = (s32[256]{0:T(256)S(1)}, s32[256]{0:T(256)}, u32[]{:S(2)}) copy-start(s32[256]{0:T(256)} %param.21) | copy-start | bytes 3076
  635.5 118.4 %all-gather.6.cloned.1.call-start = ((), (), s32[]{:S(2)}) async-start(), calls=%async_computation.3 | async-start | bytes 4128768 | tf_op jit(solution)/shard_map/all_gather | solution.py:132
  722.6 163.8 %all-gather.8.cloned.1.call-start = ((), (), s32[]{:S(2)}) async-start(), calls=%async_computation.4 | async-start | bytes 15138816 | tf_op jit(solution)/shard_map/all_gather | solution.py:137
  900.0 29.5 %copy-start.13 = (s32[256]{0:T(256)S(1)}, s32[256]{0:T(256)}, u32[]{:S(2)}) copy-start(s32[256]{0:T(256)} %param.22) | copy-start | bytes 3076
  900.0 29.5 %copy-start.16 = (s32[48]{0:T(128)S(1)}, s32[48]{0:T(128)}, u32[]{:S(2)}) copy-start(s32[48]{0:T(128)} %param.23) | copy-start | bytes 580
  900.0 29.6 %copy-start.17 = (s32[48]{0:T(128)S(1)}, s32[48]{0:T(128)}, u32[]{:S(2)}) copy-start(s32[48]{0:T(128)} %param.24) | copy-start | bytes 580
  929.5 140.7 %copy-start.14 = (f32[256]{0:T(256)}, f32[256]{0:T(256)S(1)}, u32[]{:S(2)}) copy-start(f32[256]{0:T(256)S(1)} %convert_multiply_fusion.4) | copy-start | bytes 3076
  (6 other events, 19.9 us)
Sparse Core Ops, SparseCore 0:
  10.6 94.5 all-gather.3
  635.6 83.3 reduce-scatter.1
  722.7 31.2 all-gather.5
  756.4 129.9 all-gather.7
where the time goes:
time: 1080 us
  waiting for transfers between devices  533 us (49%)
  starting transfers between devices  215 us (20%)
  blocking collectives  166 us (15%)
  other arithmetic  88.2 us (8%)
  matrix products  41 us (4%)
  local copies, waits for them, and re-layouts  18.2 us (2%)
  between operations  14.6 us (1%)
    ppermute x31, waiting for transfers between devices, shifted(): return lax.ppermute(x, axis, pairs)  220 us
    ppermute x31, starting transfers between devices, shifted(): return lax.ppermute(x, axis, pairs)  215 us
    unnamed x1, blocking collectives  139 us
    all_gather x1, waiting for transfers between devices, shards(): lax.all_gather(vocab_head_weight, 'seq', axis=0, tiled=True)  132 us
    reduce_scatter x1, waiting for transfers between devices, shards(): lax.psum_scatter(jnp.stack([base_output[:, 0] + adapter_output, base_outp...  81.4 us
    all_gather x1, waiting for transfers between devices, shards(): piece = lax.all_gather(prompt_held_states, 'seq', axis=1, tiled=True)  69.4 us
    add x31, other arithmetic, relay_step(): outgoing = carry_through[:, :, None, None] * incoming + local_end  63.3 us
    all_gather x1, waiting for transfers between devices, shards(): normed = lax.all_gather(normed_own, 'mp', axis=0, tiled=True)  28.5 us
  transfers between devices with their start and end apart: 35, of which 35 were waited for; matrix products, arithmetic and copies ran while one was open for 3% of the time, Pallas kernels for 0%

commit v1 on v0

--- a/solution.py
+++ b/solution.py
@@ -129,7 +129,10 @@
     ).astype(jnp.float32)
     own_rows = lax.dynamic_slice_in_dim(residual, lax.axis_index("mp") * share_rows, share_rows, 0)
     normed_own = root_norm(own_rows.astype(jnp.float32) + mixed, final_norm_scale)
-    normed = lax.all_gather(normed_own, "mp", axis=0, tiled=True)
+    size = lax.axis_size("mp")
+    parts = jnp.stack([normed_own for _ in range(size)])
+    parts = lax.all_to_all(parts, "mp", split_axis=0, concat_axis=0)
+    normed = jnp.concatenate(parts, axis=0)
     vocab_local = vocab_head_weight.shape[1]
     logits = jnp.einsum(
         "tmk,kv->mtv",

time: 1080 us -> 1040 us (0.963)
  waiting for transfers between devices: 533 us -> 488 us
    all_gather x1, waiting for transfers between devices: 132 us -> 73.5 us  [shards(): lax.all_gather(vocab_head_weight, 'seq', axis=0, tiled=True)]
    all_to_all x0 -> x1, waiting for transfers between devices: none -> 41.8 us  [shards(): parts = lax.all_to_all(parts, 'mp', split_axis=0, concat_axis=0)]
    all_gather x1 -> x0, waiting for transfers between devices: 28.5 us -> none  [shards(): normed = lax.all_gather(normed_own, 'mp', axis=0, tiled=True)]
  transfers between devices with their start and end apart: 35 -> 35, of which waited for: 35 -> 35; matrix products, arithmetic and copies ran while one was open for 3% -> 4% of each run, Pallas kernels for 0% -> 0%
where the time goes in v1:
time: 1040 us
  waiting for transfers between devices  488 us (47%)
  starting transfers between devices  220 us (21%)
  blocking collectives  166 us (16%)
  other arithmetic  86.6 us (8%)
  matrix products  40.8 us (4%)
  local copies, waits for them, and re-layouts  24.1 us (2%)
  between operations  14.6 us (1%)
    ppermute x31, waiting for transfers between devices, shifted(): return lax.ppermute(x, axis, pairs)  220 us
    ppermute x31, starting transfers between devices, shifted(): return lax.ppermute(x, axis, pairs)  215 us
    unnamed x1, blocking collectives  139 us
    reduce_scatter x1, waiting for transfers between devices, shards(): lax.psum_scatter(jnp.stack([base_output[:, 0] + adapter_output, base_outp...  81.5 us
    all_gather x1, waiting for transfers between devices, shards(): lax.all_gather(vocab_head_weight, 'seq', axis=0, tiled=True)  73.5 us
    all_gather x1, waiting for transfers between devices, shards(): piece = lax.all_gather(prompt_held_states, 'seq', axis=1, tiled=True)  69.4 us
    add x31, other arithmetic, relay_step(): outgoing = carry_through[:, :, None, None] * incoming + local_end  63.3 us
    all_to_all x1, waiting for transfers between devices, shards(): parts = lax.all_to_all(parts, 'mp', split_axis=0, concat_axis=0)  41.8 us
  transfers between devices with their start and end apart: 35, of which 35 were waited for; matrix products, arithmetic and copies ran while one was open for 4% of the time, Pallas kernels for 0%

profile of v1, /device:TPU:0, one launch (start us, length us, event | category | flops | bytes accessed | tf_op | source)
XLA Modules:
  0.0 1040.0 jit_solution(1614898430696935011)
XLA Ops:
  35.8 69.4 %all-gather.3.cloned.1.call-done = bf16[2,32,7,64,64]{4,3,1,2,0:T(8,128)(2,1)} async-done(((bf16[2,1,7,64,64]{4,3,1,2,0:T(8,128)(2,1)}), bf16[2,32,7,64,64]{4,3,1,2,0:T(8,128)(2,1)}) %all-gather.3.cloned.1.call-update) | async-done | bytes 3670032 | tf_op jit(solution)/shard_map/all_gather | solution.py:81
  105.2 7.4 fusion.2
  117.8 498.9 %while.10 = (s32[]{:T(128)}, f32[2,7,64,64]{3,2,1,0:T(8,128)}, f32[2,7]{1,0:T(2,128)S(1)}, f32[2,7,64,64]{3,2,1,0:T(8,128)}, s32[]{:T(128)}) while((s32[]{:T(128)}, f32[2,7,64,64]{3,2,1,0:T(8,128)}, f32[2,7]{1,0:T(2,128)S(1)}, f32[2,7,64,64]{3,2,1,0:T(8,128)}, s32[]{:T(128)}) %tuple.33), condition=%wide.region_7.8_spmd, body=%wide.region_6.7_spmd.sunk | while | flops 114690 | bytes 1605789 | solution.py:102
  122.8 8.9 collective-permute-done
  138.9 7.9 collective-permute-done
  154.1 7.0 collective-permute-done
  215.3 7.3 collective-permute-start
  230.1 7.5 collective-permute-start
  246.1 7.9 collective-permute-start
  254.0 7.5 collective-permute-done
  263.5 8.2 collective-permute-start
  271.7 8.6 collective-permute-done
  282.4 8.2 collective-permute-start
  290.5 9.8 collective-permute-done
  302.4 8.2 collective-permute-start
  310.6 9.9 collective-permute-done
  322.5 7.6 collective-permute-start
  330.1 8.7 collective-permute-done
  347.2 7.4 collective-permute-done
  356.7 7.3 collective-permute-start
  372.5 7.3 collective-permute-start
  387.4 7.3 collective-permute-start
  402.3 7.3 collective-permute-start
  417.1 7.3 collective-permute-start
  431.9 7.3 collective-permute-start
  446.8 7.3 collective-permute-start
  462.2 7.6 collective-permute-start
  469.8 7.1 collective-permute-done
  479.0 8.2 collective-permute-start
  487.1 8.2 collective-permute-done
  497.4 8.2 collective-permute-start
  505.6 9.3 collective-permute-done
  517.0 8.2 collective-permute-start
  525.2 10.3 collective-permute-done
  537.5 7.6 collective-permute-start
  545.1 9.1 collective-permute-done
  556.3 7.1 collective-permute-start
  563.4 8.0 collective-permute-done
  580.2 6.9 collective-permute-done
  589.1 7.3 collective-permute-start
  603.9 7.3 collective-permute-start
  636.5 81.5 %reduce-scatter.2.cloned.1.call-done = bf16[32,2,3584]{2,0,1:T(8,128)(2,1)} async-done(((bf16[256,2,3584]{2,0,1:T(8,128)(2,1)}), bf16[32,2,3584]{2,0,1:T(8,128)(2,1)}) %reduce-scatter.2.cloned.1.call-update) | async-done | bytes 458768 | tf_op jit(solution)/shard_map/reduce_scatter | solution.py:122
  729.6 41.8 %all-to-all-done = bf16[8,32,2,3584]{3,1,2,0:T(8,128)(2,1)} async-done(((bf16[8,32,2,3584]{3,1,2,0:T(8,128)(2,1)}), bf16[8,32,2,3584]{3,1,2,0:T(8,128)(2,1)}, u32[]{:S(2)}, u32[]{:S(2)}) %all-to-all-start) | async-done | bytes 3670048 | tf_op jit(solution)/shard_map/all_to_all | solution.py:134
  776.0 73.5 %all-gather.5.cloned.1.call-done = bf16[3584,2000]{1,0:T(8,128)(2,1)} async-done(((bf16[112,2000]{1,0:T(8,128)(2,1)}), bf16[3584,2000]{1,0:T(8,128)(2,1)}) %all-gather.5.cloned.1.call-update) | async-done | bytes 14336016 | tf_op jit(solution)/shard_map/all_gather | solution.py:140
  849.6 13.8 %fusion.6 = (f32[2,256]{1,0:T(2,128)S(1)}, f32[2,256]{1,0:T(2,128)S(1)}, f32[256,2,2000]{0,2,1:T(8,128)}) fusion(pred[256,2000]{0,1:T(8,128)(4,1)} %broadcast_compare_fusion, bf16[256,2,3584]{2,0,1:T(8,128)(2,1)} %bitcast.119, bf16[3584,2000]{1,0:T(8,128)(2,1)} %all-gather.5.cloned.1.call-done), kind=kOutput, calls=%fused_computation.14 | convolution fusion | flops 7343102976 | bytes 22618112 | tf_op jit(solution)/shard_map/tmk,kv->mtv/dot_general | solution.py:137
  863.4 14.3 %pmax.7 = f32[2,256]{1,0:T(2,128)S(1)} all-reduce(f32[2,256]{1,0:T(2,128)S(1)} %get-tuple-element.26), channel_id=1, replica_groups=mesh['seq'=32,'mp'=8] {'mp'}, use_global_device_ids=true, to_apply=%region_13.14 | all-reduce | flops 512 | bytes 4096 | tf_op jit(solution)/shard_map/pmax | solution.py:150
  880.4 12.4 %all-reduce.1 = (f32[2,256]{1,0:T(2,128)S(1)}, f32[2,256]{1,0:T(2,128)S(1)}) all-reduce(f32[2,256]{1,0:T(2,128)S(1)} %fusion.8, f32[2,256]{1,0:T(2,128)S(1)} %get-tuple-element.25), channel_id=1, replica_groups=mesh['seq'=32,'mp'=8] {'mp'}, use_global_device_ids=true, to_apply=%region_15.16 | all-reduce | flops 1024 | bytes 8192 | tf_op jit(solution)/shard_map/psum | solution.py:152
  893.0 139.3 %all-reduce = f32[32,48]{1,0:T(8,128)S(1)} all-reduce(f32[32,48]{1,0:T(8,128)S(1)} %fusion.54), channel_id=3, replica_groups=mesh['seq'=32,'mp'=8] {'seq'}, use_global_device_ids=true, to_apply=%region_16.17.clone | all-reduce | flops 1536 | bytes 12288
  (180 shorter events, 270.1 us)
Async XLA Ops:
  7.2 613.0 %copy-start = (bf16[448,3584]{1,0:T(8,128)(2,1)S(1)}, bf16[448,3584]{1,0:T(8,128)(2,1)}, u32[]{:S(2)}) copy-start(bf16[448,3584]{1,0:T(8,128)(2,1)} %param.34) | copy-start | bytes 9633796
  7.2 98.0 %all-gather.3.cloned.1.call-start = ((), (), s32[]{:S(2)}) async-start(), calls=%async_computation.2 | async-start | bytes 7569408 | tf_op jit(solution)/shard_map/all_gather | solution.py:81
  7.9 710.1 %reduce-scatter.2.cloned.1.call-start = ((), (), s32[]{:S(2)}) async-start(), calls=%async_computation.3 | async-start | bytes 4128768 | tf_op jit(solution)/shard_map/reduce_scatter | solution.py:122
  30.4 82.1 %copy-start.10 = (bf16[2,256,64]{1,2,0:T(8,128)(2,1)S(1)}, bf16[2,256,64]{1,2,0:T(8,128)(2,1)}, u32[]{:S(2)}) copy-start(bf16[2,256,64]{1,2,0:T(8,128)(2,1)} %param.28) | copy-start | bytes 196612
  105.2 7.4 copy-start.6
  105.2 8.8 copy-start.3
  105.2 8.8 copy-start.13
  117.0 499.8 %copy-start.8 = (bf16[2,256,64]{1,2,0:T(8,128)(2,1)S(1)}, bf16[2,256,64]{1,2,0:T(8,128)(2,1)}, u32[]{:S(2)}) copy-start(bf16[2,256,64]{1,2,0:T(8,128)(2,1)} %param.29) | copy-start | bytes 196612
  117.0 499.8 %copy-start.18 = (f32[2,7]{1,0:T(2,128)S(1)}, f32[2,7]{1,0:T(2,128)}, u32[]{:S(2)}) copy-start(f32[2,7]{1,0:T(2,128)} %param.32) | copy-start | bytes 172
  119.9 11.8 %collective-permute-start = (f32[2,7,64,64]{3,2,1,0:T(8,128)}, f32[2,7,64,64]{3,2,1,0:T(8,128)}, u32[]{:S(2)}, u32[]{:S(2)}) collective-permute-start(f32[2,7,64,64]{3,2,1,0:T(8,128)} %multiply_add_fusion.2), channel_id=1, source_target_pairs={{0,8},{8,16},{16,24},{24,32},{32,40},{40,48},{48,56},{56,64},{64,7... | collective-permute-start | bytes 688136 | tf_op jit(solution)/shard_map/while/body/eval_jaxpr/ppermute | solution.py:12
  133.7 13.1 %collective-permute-start = (f32[2,7,64,64]{3,2,1,0:T(8,128)}, f32[2,7,64,64]{3,2,1,0:T(8,128)}, u32[]{:S(2)}, u32[]{:S(2)}) collective-permute-start(f32[2,7,64,64]{3,2,1,0:T(8,128)} %multiply_add_fusion.2), channel_id=1, source_target_pairs={{0,8},{8,16},{16,24},{24,32},{32,40},{40,48},{48,56},{56,64},{64,7... | collective-permute-start | bytes 688136 | tf_op jit(solution)/shard_map/while/body/eval_jaxpr/ppermute | solution.py:12
  148.9 12.2 %collective-permute-start = (f32[2,7,64,64]{3,2,1,0:T(8,128)}, f32[2,7,64,64]{3,2,1,0:T(8,128)}, u32[]{:S(2)}, u32[]{:S(2)}) collective-permute-start(f32[2,7,64,64]{3,2,1,0:T(8,128)} %multiply_add_fusion.2), channel_id=1, source_target_pairs={{0,8},{8,16},{16,24},{24,32},{32,40},{40,48},{48,56},{56,64},{64,7... | collective-permute-start | bytes 688136 | tf_op jit(solution)/shard_map/while/body/eval_jaxpr/ppermute | solution.py:12
  163.1 11.3 %collective-permute-start = (f32[2,7,64,64]{3,2,1,0:T(8,128)}, f32[2,7,64,64]{3,2,1,0:T(8,128)}, u32[]{:S(2)}, u32[]{:S(2)}) collective-permute-start(f32[2,7,64,64]{3,2,1,0:T(8,128)} %multiply_add_fusion.2), channel_id=1, source_target_pairs={{0,8},{8,16},{16,24},{24,32},{32,40},{40,48},{48,56},{56,64},{64,7... | collective-permute-start | bytes 688136 | tf_op jit(solution)/shard_map/while/body/eval_jaxpr/ppermute | solution.py:12
  176.5 10.7 %collective-permute-start = (f32[2,7,64,64]{3,2,1,0:T(8,128)}, f32[2,7,64,64]{3,2,1,0:T(8,128)}, u32[]{:S(2)}, u32[]{:S(2)}) collective-permute-start(f32[2,7,64,64]{3,2,1,0:T(8,128)} %multiply_add_fusion.2), channel_id=1, source_target_pairs={{0,8},{8,16},{16,24},{24,32},{32,40},{40,48},{48,56},{56,64},{64,7... | collective-permute-start | bytes 688136 | tf_op jit(solution)/shard_map/while/body/eval_jaxpr/ppermute | solution.py:12
  189.2 10.7 %collective-permute-start = (f32[2,7,64,64]{3,2,1,0:T(8,128)}, f32[2,7,64,64]{3,2,1,0:T(8,128)}, u32[]{:S(2)}, u32[]{:S(2)}) collective-permute-start(f32[2,7,64,64]{3,2,1,0:T(8,128)} %multiply_add_fusion.2), channel_id=1, source_target_pairs={{0,8},{8,16},{16,24},{24,32},{32,40},{40,48},{48,56},{56,64},{64,7... | collective-permute-start | bytes 688136 | tf_op jit(solution)/shard_map/while/body/eval_jaxpr/ppermute | solution.py:12
  201.9 11.4 %collective-permute-start = (f32[2,7,64,64]{3,2,1,0:T(8,128)}, f32[2,7,64,64]{3,2,1,0:T(8,128)}, u32[]{:S(2)}, u32[]{:S(2)}) collective-permute-start(f32[2,7,64,64]{3,2,1,0:T(8,128)} %multiply_add_fusion.2), channel_id=1, source_target_pairs={{0,8},{8,16},{16,24},{24,32},{32,40},{40,48},{48,56},{56,64},{64,7... | collective-permute-start | bytes 688136 | tf_op jit(solution)/shard_map/while/body/eval_jaxpr/ppermute | solution.py:12
  215.3 12.8 %collective-permute-start = (f32[2,7,64,64]{3,2,1,0:T(8,128)}, f32[2,7,64,64]{3,2,1,0:T(8,128)}, u32[]{:S(2)}, u32[]{:S(2)}) collective-permute-start(f32[2,7,64,64]{3,2,1,0:T(8,128)} %multiply_add_fusion.2), channel_id=1, source_target_pairs={{0,8},{8,16},{16,24},{24,32},{32,40},{40,48},{48,56},{56,64},{64,7... | collective-permute-start | bytes 688136 | tf_op jit(solution)/shard_map/while/body/eval_jaxpr/ppermute | solution.py:12
  230.1 13.9 %collective-permute-start = (f32[2,7,64,64]{3,2,1,0:T(8,128)}, f32[2,7,64,64]{3,2,1,0:T(8,128)}, u32[]{:S(2)}, u32[]{:S(2)}) collective-permute-start(f32[2,7,64,64]{3,2,1,0:T(8,128)} %multiply_add_fusion.2), channel_id=1, source_target_pairs={{0,8},{8,16},{16,24},{24,32},{32,40},{40,48},{48,56},{56,64},{64,7... | collective-permute-start | bytes 688136 | tf_op jit(solution)/shard_map/while/body/eval_jaxpr/ppermute | solution.py:12
  246.1 15.4 %collective-permute-start = (f32[2,7,64,64]{3,2,1,0:T(8,128)}, f32[2,7,64,64]{3,2,1,0:T(8,128)}, u32[]{:S(2)}, u32[]{:S(2)}) collective-permute-start(f32[2,7,64,64]{3,2,1,0:T(8,128)} %multiply_add_fusion.2), channel_id=1, source_target_pairs={{0,8},{8,16},{16,24},{24,32},{32,40},{40,48},{48,56},{56,64},{64,7... | collective-permute-start | bytes 688136 | tf_op jit(solution)/shard_map/while/body/eval_jaxpr/ppermute | solution.py:12
  263.5 16.8 %collective-permute-start = (f32[2,7,64,64]{3,2,1,0:T(8,128)}, f32[2,7,64,64]{3,2,1,0:T(8,128)}, u32[]{:S(2)}, u32[]{:S(2)}) collective-permute-start(f32[2,7,64,64]{3,2,1,0:T(8,128)} %multiply_add_fusion.2), channel_id=1, source_target_pairs={{0,8},{8,16},{16,24},{24,32},{32,40},{40,48},{48,56},{56,64},{64,7... | collective-permute-start | bytes 688136 | tf_op jit(solution)/shard_map/while/body/eval_jaxpr/ppermute | solution.py:12
  282.4 18.0 %collective-permute-start = (f32[2,7,64,64]{3,2,1,0:T(8,128)}, f32[2,7,64,64]{3,2,1,0:T(8,128)}, u32[]{:S(2)}, u32[]{:S(2)}) collective-permute-start(f32[2,7,64,64]{3,2,1,0:T(8,128)} %multiply_add_fusion.2), channel_id=1, source_target_pairs={{0,8},{8,16},{16,24},{24,32},{32,40},{40,48},{48,56},{56,64},{64,7... | collective-permute-start | bytes 688136 | tf_op jit(solution)/shard_map/while/body/eval_jaxpr/ppermute | solution.py:12
  302.4 18.1 %collective-permute-start = (f32[2,7,64,64]{3,2,1,0:T(8,128)}, f32[2,7,64,64]{3,2,1,0:T(8,128)}, u32[]{:S(2)}, u32[]{:S(2)}) collective-permute-start(f32[2,7,64,64]{3,2,1,0:T(8,128)} %multiply_add_fusion.2), channel_id=1, source_target_pairs={{0,8},{8,16},{16,24},{24,32},{32,40},{40,48},{48,56},{56,64},{64,7... | collective-permute-start | bytes 688136 | tf_op jit(solution)/shard_map/while/body/eval_jaxpr/ppermute | solution.py:12
  322.5 16.2 %collective-permute-start = (f32[2,7,64,64]{3,2,1,0:T(8,128)}, f32[2,7,64,64]{3,2,1,0:T(8,128)}, u32[]{:S(2)}, u32[]{:S(2)}) collective-permute-start(f32[2,7,64,64]{3,2,1,0:T(8,128)} %multiply_add_fusion.2), channel_id=1, source_target_pairs={{0,8},{8,16},{16,24},{24,32},{32,40},{40,48},{48,56},{56,64},{64,7... | collective-permute-start | bytes 688136 | tf_op jit(solution)/shard_map/while/body/eval_jaxpr/ppermute | solution.py:12
  340.8 13.8 %collective-permute-start = (f32[2,7,64,64]{3,2,1,0:T(8,128)}, f32[2,7,64,64]{3,2,1,0:T(8,128)}, u32[]{:S(2)}, u32[]{:S(2)}) collective-permute-start(f32[2,7,64,64]{3,2,1,0:T(8,128)} %multiply_add_fusion.2), channel_id=1, source_target_pairs={{0,8},{8,16},{16,24},{24,32},{32,40},{40,48},{48,56},{56,64},{64,7... | collective-permute-start | bytes 688136 | tf_op jit(solution)/shard_map/while/body/eval_jaxpr/ppermute | solution.py:12
  356.7 13.8 %collective-permute-start = (f32[2,7,64,64]{3,2,1,0:T(8,128)}, f32[2,7,64,64]{3,2,1,0:T(8,128)}, u32[]{:S(2)}, u32[]{:S(2)}) collective-permute-start(f32[2,7,64,64]{3,2,1,0:T(8,128)} %multiply_add_fusion.2), channel_id=1, source_target_pairs={{0,8},{8,16},{16,24},{24,32},{32,40},{40,48},{48,56},{56,64},{64,7... | collective-permute-start | bytes 688136 | tf_op jit(solution)/shard_map/while/body/eval_jaxpr/ppermute | solution.py:12
  372.5 12.9 %collective-permute-start = (f32[2,7,64,64]{3,2,1,0:T(8,128)}, f32[2,7,64,64]{3,2,1,0:T(8,128)}, u32[]{:S(2)}, u32[]{:S(2)}) collective-permute-start(f32[2,7,64,64]{3,2,1,0:T(8,128)} %multiply_add_fusion.2), channel_id=1, source_target_pairs={{0,8},{8,16},{16,24},{24,32},{32,40},{40,48},{48,56},{56,64},{64,7... | collective-permute-start | bytes 688136 | tf_op jit(solution)/shard_map/while/body/eval_jaxpr/ppermute | solution.py:12
  387.4 12.8 %collective-permute-start = (f32[2,7,64,64]{3,2,1,0:T(8,128)}, f32[2,7,64,64]{3,2,1,0:T(8,128)}, u32[]{:S(2)}, u32[]{:S(2)}) collective-permute-start(f32[2,7,64,64]{3,2,1,0:T(8,128)} %multiply_add_fusion.2), channel_id=1, source_target_pairs={{0,8},{8,16},{16,24},{24,32},{32,40},{40,48},{48,56},{56,64},{64,7... | collective-permute-start | bytes 688136 | tf_op jit(solution)/shard_map/while/body/eval_jaxpr/ppermute | solution.py:12
  402.3 12.8 %collective-permute-start = (f32[2,7,64,64]{3,2,1,0:T(8,128)}, f32[2,7,64,64]{3,2,1,0:T(8,128)}, u32[]{:S(2)}, u32[]{:S(2)}) collective-permute-start(f32[2,7,64,64]{3,2,1,0:T(8,128)} %multiply_add_fusion.2), channel_id=1, source_target_pairs={{0,8},{8,16},{16,24},{24,32},{32,40},{40,48},{48,56},{56,64},{64,7... | collective-permute-start | bytes 688136 | tf_op jit(solution)/shard_map/while/body/eval_jaxpr/ppermute | solution.py:12
  417.1 12.8 %collective-permute-start = (f32[2,7,64,64]{3,2,1,0:T(8,128)}, f32[2,7,64,64]{3,2,1,0:T(8,128)}, u32[]{:S(2)}, u32[]{:S(2)}) collective-permute-start(f32[2,7,64,64]{3,2,1,0:T(8,128)} %multiply_add_fusion.2), channel_id=1, source_target_pairs={{0,8},{8,16},{16,24},{24,32},{32,40},{40,48},{48,56},{56,64},{64,7... | collective-permute-start | bytes 688136 | tf_op jit(solution)/shard_map/while/body/eval_jaxpr/ppermute | solution.py:12
  431.9 12.8 %collective-permute-start = (f32[2,7,64,64]{3,2,1,0:T(8,128)}, f32[2,7,64,64]{3,2,1,0:T(8,128)}, u32[]{:S(2)}, u32[]{:S(2)}) collective-permute-start(f32[2,7,64,64]{3,2,1,0:T(8,128)} %multiply_add_fusion.2), channel_id=1, source_target_pairs={{0,8},{8,16},{16,24},{24,32},{32,40},{40,48},{48,56},{56,64},{64,7... | collective-permute-start | bytes 688136 | tf_op jit(solution)/shard_map/while/body/eval_jaxpr/ppermute | solution.py:12
  446.8 13.4 %collective-permute-start = (f32[2,7,64,64]{3,2,1,0:T(8,128)}, f32[2,7,64,64]{3,2,1,0:T(8,128)}, u32[]{:S(2)}, u32[]{:S(2)}) collective-permute-start(f32[2,7,64,64]{3,2,1,0:T(8,128)} %multiply_add_fusion.2), channel_id=1, source_target_pairs={{0,8},{8,16},{16,24},{24,32},{32,40},{40,48},{48,56},{56,64},{64,7... | collective-permute-start | bytes 688136 | tf_op jit(solution)/shard_map/while/body/eval_jaxpr/ppermute | solution.py:12
  462.2 14.7 %collective-permute-start = (f32[2,7,64,64]{3,2,1,0:T(8,128)}, f32[2,7,64,64]{3,2,1,0:T(8,128)}, u32[]{:S(2)}, u32[]{:S(2)}) collective-permute-start(f32[2,7,64,64]{3,2,1,0:T(8,128)} %multiply_add_fusion.2), channel_id=1, source_target_pairs={{0,8},{8,16},{16,24},{24,32},{32,40},{40,48},{48,56},{56,64},{64,7... | collective-permute-start | bytes 688136 | tf_op jit(solution)/shard_map/while/body/eval_jaxpr/ppermute | solution.py:12
  479.0 16.4 %collective-permute-start = (f32[2,7,64,64]{3,2,1,0:T(8,128)}, f32[2,7,64,64]{3,2,1,0:T(8,128)}, u32[]{:S(2)}, u32[]{:S(2)}) collective-permute-start(f32[2,7,64,64]{3,2,1,0:T(8,128)} %multiply_add_fusion.2), channel_id=1, source_target_pairs={{0,8},{8,16},{16,24},{24,32},{32,40},{40,48},{48,56},{56,64},{64,7... | collective-permute-start | bytes 688136 | tf_op jit(solution)/shard_map/while/body/eval_jaxpr/ppermute | solution.py:12
  497.4 17.5 %collective-permute-start = (f32[2,7,64,64]{3,2,1,0:T(8,128)}, f32[2,7,64,64]{3,2,1,0:T(8,128)}, u32[]{:S(2)}, u32[]{:S(2)}) collective-permute-start(f32[2,7,64,64]{3,2,1,0:T(8,128)} %multiply_add_fusion.2), channel_id=1, source_target_pairs={{0,8},{8,16},{16,24},{24,32},{32,40},{40,48},{48,56},{56,64},{64,7... | collective-permute-start | bytes 688136 | tf_op jit(solution)/shard_map/while/body/eval_jaxpr/ppermute | solution.py:12
  517.0 18.5 %collective-permute-start = (f32[2,7,64,64]{3,2,1,0:T(8,128)}, f32[2,7,64,64]{3,2,1,0:T(8,128)}, u32[]{:S(2)}, u32[]{:S(2)}) collective-permute-start(f32[2,7,64,64]{3,2,1,0:T(8,128)} %multiply_add_fusion.2), channel_id=1, source_target_pairs={{0,8},{8,16},{16,24},{24,32},{32,40},{40,48},{48,56},{56,64},{64,7... | collective-permute-start | bytes 688136 | tf_op jit(solution)/shard_map/while/body/eval_jaxpr/ppermute | solution.py:12
  537.5 16.7 %collective-permute-start = (f32[2,7,64,64]{3,2,1,0:T(8,128)}, f32[2,7,64,64]{3,2,1,0:T(8,128)}, u32[]{:S(2)}, u32[]{:S(2)}) collective-permute-start(f32[2,7,64,64]{3,2,1,0:T(8,128)} %multiply_add_fusion.2), channel_id=1, source_target_pairs={{0,8},{8,16},{16,24},{24,32},{32,40},{40,48},{48,56},{56,64},{64,7... | collective-permute-start | bytes 688136 | tf_op jit(solution)/shard_map/while/body/eval_jaxpr/ppermute | solution.py:12
  556.3 15.0 %collective-permute-start = (f32[2,7,64,64]{3,2,1,0:T(8,128)}, f32[2,7,64,64]{3,2,1,0:T(8,128)}, u32[]{:S(2)}, u32[]{:S(2)}) collective-permute-start(f32[2,7,64,64]{3,2,1,0:T(8,128)} %multiply_add_fusion.2), channel_id=1, source_target_pairs={{0,8},{8,16},{16,24},{24,32},{32,40},{40,48},{48,56},{56,64},{64,7... | collective-permute-start | bytes 688136 | tf_op jit(solution)/shard_map/while/body/eval_jaxpr/ppermute | solution.py:12
  573.4 13.7 %collective-permute-start = (f32[2,7,64,64]{3,2,1,0:T(8,128)}, f32[2,7,64,64]{3,2,1,0:T(8,128)}, u32[]{:S(2)}, u32[]{:S(2)}) collective-permute-start(f32[2,7,64,64]{3,2,1,0:T(8,128)} %multiply_add_fusion.2), channel_id=1, source_target_pairs={{0,8},{8,16},{16,24},{24,32},{32,40},{40,48},{48,56},{56,64},{64,7... | collective-permute-start | bytes 688136 | tf_op jit(solution)/shard_map/while/body/eval_jaxpr/ppermute | solution.py:12
  589.1 12.8 %collective-permute-start = (f32[2,7,64,64]{3,2,1,0:T(8,128)}, f32[2,7,64,64]{3,2,1,0:T(8,128)}, u32[]{:S(2)}, u32[]{:S(2)}) collective-permute-start(f32[2,7,64,64]{3,2,1,0:T(8,128)} %multiply_add_fusion.2), channel_id=1, source_target_pairs={{0,8},{8,16},{16,24},{24,32},{32,40},{40,48},{48,56},{56,64},{64,7... | collective-permute-start | bytes 688136 | tf_op jit(solution)/shard_map/while/body/eval_jaxpr/ppermute | solution.py:12
  603.9 12.8 %collective-permute-start = (f32[2,7,64,64]{3,2,1,0:T(8,128)}, f32[2,7,64,64]{3,2,1,0:T(8,128)}, u32[]{:S(2)}, u32[]{:S(2)}) collective-permute-start(f32[2,7,64,64]{3,2,1,0:T(8,128)} %multiply_add_fusion.2), channel_id=1, source_target_pairs={{0,8},{8,16},{16,24},{24,32},{32,40},{40,48},{48,56},{56,64},{64,7... | collective-permute-start | bytes 688136 | tf_op jit(solution)/shard_map/while/body/eval_jaxpr/ppermute | solution.py:12
  634.4 84.8 %copy-start.12 = (f32[3584]{0:T(1024)S(1)}, f32[3584]{0:T(1024)}, u32[]{:S(2)}) copy-start(f32[3584]{0:T(1024)} %param.38) | copy-start | bytes 43012
  634.5 215.1 %all-gather.5.cloned.1.call-start = ((), (), s32[]{:S(2)}) async-start(), calls=%async_computation.4 | async-start | bytes 15138816 | tf_op jit(solution)/shard_map/all_gather | solution.py:140
  722.6 48.7 %all-to-all-start = ((bf16[8,32,2,3584]{3,1,2,0:T(8,128)(2,1)}), bf16[8,32,2,3584]{3,1,2,0:T(8,128)(2,1)}, u32[]{:S(2)}, u32[]{:S(2)}) async-start(bf16[8,32,2,3584]{3,1,2,0:T(8,128)(2,1)} %stack.10), calls=%async_computation.1 | async-start | bytes 7340032 | tf_op jit(solution)/shard_map/all_to_all | solution.py:134
  849.6 183.9 %copy-start.1 = (bf16[448,3584]{1,0:T(8,128)(2,1)S(1)}, bf16[448,3584]{1,0:T(8,128)(2,1)}, u32[]{:S(2)}) copy-start(bf16[448,3584]{1,0:T(8,128)(2,1)} %param.34) | copy-start | bytes 9633796
  863.3 29.5 %copy-start.16 = (s32[256]{0:T(256)S(1)}, s32[256]{0:T(256)}, u32[]{:S(2)}) copy-start(s32[256]{0:T(256)} %param.22) | copy-start | bytes 3076
  863.3 29.5 %copy-start.19 = (s32[48]{0:T(128)S(1)}, s32[48]{0:T(128)}, u32[]{:S(2)}) copy-start(s32[48]{0:T(128)} %param.23) | copy-start | bytes 580
  863.3 29.6 %copy-start.20 = (s32[48]{0:T(128)S(1)}, s32[48]{0:T(128)}, u32[]{:S(2)}) copy-start(s32[48]{0:T(128)} %param.24) | copy-start | bytes 580
  892.8 140.7 %copy-start.17 = (f32[256]{0:T(256)}, f32[256]{0:T(256)S(1)}, u32[]{:S(2)}) copy-start(f32[256]{0:T(256)S(1)} %convert_multiply_fusion.4) | copy-start | bytes 3076
  (9 other events, 24.6 us)
Sparse Core Ops, SparseCore 0:
  10.6 94.5 all-gather.2
  634.6 83.3 reduce-scatter.1
  720.6 128.9 all-gather.4
